TPU v7x, 128 devices: a whole 4x4x4 slice. The times are simulated.
128 devices in a mesh: leaf: 64 (over y_hi, x, z, core), rhs: 2 (over y_lo).
Axes of the slice: x: 4, y: 4 (y_hi: 2, y_lo: 2; y = y_hi * 2 + y_lo), z: 4, core: 2. Of those that a mesh axis runs over, the one named last changes fastest.
Arguments:
- rhs: bfloat16 [524288, 512], P('leaf', 'rhs'), may hold values from -6 to 6
- source_basis: bfloat16 [4096, 128, 128], P('leaf', None, 'rhs'), may hold values from -0.5 to 0.5
- target_basis: bfloat16 [4096, 128, 128], P('leaf', None, 'rhs'), may hold values from -0.5 to 0.5
- near_blocks: bfloat16 [4096, 2, 128, 128], P('leaf', None, None, 'rhs'), may hold values from -0.375 to 0.375
- near_offsets: int32 [4096, 2], P('leaf'), may hold values from -2 to 2
- source_values: bfloat16 [3, 2048, 2, 2, 128, 128], P(None, 'leaf', None, None, 'rhs'), may hold values from -0.375 to 0.375
- source_scales: float32 [3, 2048, 2, 2, 128], P(None, 'leaf'), may hold values from 0.2 to 2
- target_values: bfloat16 [3, 2048, 2, 2, 128, 128], P(None, 'leaf', None, None, 'rhs'), may hold values from -0.375 to 0.375
- target_scales: float32 [3, 2048, 2, 2, 128], P(None, 'leaf'), may hold values from 0.2 to 2
Outputs:
- product: bfloat16 [524288, 512], P('leaf', 'rhs')
All inputs are finite; a program needn't handle non-finite values.
Results may differ from a plain program's by a relative error of at most 0.01.
Values may be sent and summed in bfloat16 or wider, within the bound.
A program may use at most 192 MiB of HBM per device.

v0:
```python
import jax
import jax.numpy as jnp
from jax import lax
from jax.sharding import PartitionSpec as P

REACH = 2
SRC_LEVELS = 3
TGT_LEVELS = 3


def padded_2(cells, sides, width):
    for axis, dim in sides:
        count = lax.axis_size(axis)
        ends = count - 1
        head = lax.slice_in_dim(cells, 0, width, axis=dim)
        tail = lax.slice_in_dim(cells, cells.shape[dim] - width, cells.shape[dim], axis=dim)
        cells = jnp.concatenate(
            [
                lax.ppermute(tail, axis, [(i, (i + 1) % count) for i in range(ends)]),
                cells,
                lax.ppermute(head, axis, [((i + 1) % count, i) for i in range(ends)]),
            ],
            axis=dim,
        )
    return cells


def dequantize(values, scales):
    return (values.astype(jnp.float32) * scales[..., None, :]).astype(jnp.bfloat16)


def butterfly_level(coefficients, blocks, bit_index):
    box_total, columns, rank = coefficients.shape
    outputs = blocks.shape[-2]
    low_span = 2**bit_index
    high_span = box_total // (2 * low_span)
    inputs = coefficients.reshape(high_span, 2, low_span, columns, rank)
    matrices = blocks.reshape(high_span, low_span, 2, 2, outputs, rank)
    mixed = jnp.einsum("hclnr,hlocsr->holns", inputs, matrices, preferred_element_type=jnp.float32)
    return mixed.reshape(box_total, columns, outputs).astype(jnp.bfloat16)


def apply_level(coefficients, scales, bit_index, gathered):
    return butterfly_level(coefficients, dequantize(gathered, scales), bit_index)


def on_device(
    rhs,
    source_basis,
    target_basis,
    near_blocks,
    near_offsets,
    source_values,
    source_scales,
    target_values,
    target_scales,
):
    box_count = source_basis.shape[0]
    box_rows = source_basis.shape[1]
    columns = rhs.shape[1]
    rhs_boxes = rhs.reshape(box_count, box_rows, columns)
    basis_in, basis_out, near_full = (
        lax.all_gather(source_basis, "rhs", axis=2, tiled=True),
        lax.all_gather(target_basis, "rhs", axis=2, tiled=True),
        lax.all_gather(near_blocks, "rhs", axis=3, tiled=True),
    )
    source_tables, target_tables = (
        lax.all_gather(source_values, "rhs", axis=4, tiled=True),
        lax.all_gather(target_values, "rhs", axis=4, tiled=True),
    )
    coefficients = jnp.einsum(
        "bmc,bmr->bcr", rhs_boxes, basis_in, preferred_element_type=jnp.float32
    ).astype(jnp.bfloat16)
    for level_index in range(SRC_LEVELS):
        coefficients = apply_level(
            coefficients, source_scales[level_index], level_index, source_tables[level_index]
        )
    padded = padded_2(rhs_boxes, (("leaf", 0),), REACH)
    source_index = jnp.arange(box_count, dtype=jnp.int32)[:, None] + REACH + near_offsets
    selected = jnp.take(padded, source_index, axis=0)
    near_field = jnp.einsum(
        "bkmn,bknc->bmc", near_full, selected, preferred_element_type=jnp.float32
    )
    row_coefficients = lax.all_to_all(coefficients, "leaf", split_axis=0, concat_axis=0, tiled=True)
    for level_index in range(TGT_LEVELS):
        row_coefficients = apply_level(
            row_coefficients, target_scales[level_index], level_index, target_tables[level_index]
        )
    far_field = jnp.einsum(
        "bmr,bcr->bmc", basis_out, row_coefficients, preferred_element_type=jnp.float32
    )
    return (far_field + near_field).astype(jnp.bfloat16).reshape(box_count * box_rows, columns)


def solution(mesh):
    placed = (
        P("leaf", "rhs"),
        P("leaf", None, "rhs"),
        P("leaf", None, "rhs"),
        P("leaf", None, None, "rhs"),
        P("leaf", None),
        P(None, "leaf", None, None, "rhs", None),
        P(None, "leaf", None, None, None),
        P(None, "leaf", None, None, "rhs", None),
        P(None, "leaf", None, None, None),
    )
    return jax.shard_map(
        on_device, mesh=mesh, in_specs=placed, out_specs=P("leaf", "rhs"), check_vma=False
    )
```

profile of v0, /device:TPU:1, one launch (start us, length us, event | category | flops | bytes accessed | tf_op | source)
XLA Modules:
  0.0 526.6 jit_solution(11540010097013420315)
XLA Ops:
  9.0 38.7 %all-gather.10.cloned.1.call-done = bf16[64,128,128]{1,2,0:T(8,128)(2,1)} async-done(((bf16[64,128,64]{1,2,0:T(8,128)(2,1)}), bf16[64,128,128]{1,2,0:T(8,128)(2,1)}) %all-gather.10.cloned.1.call-update) | async-done | bytes 2097168 | tf_op jit(solution)/shard_map/all_gather | solution.py:63
  47.7 6.2 %convolution_convert_fusion = bf16[64,256,128]{2,1,0:T(8,128)(2,1)} fusion(bf16[64,128,256]{2,1,0:T(8,128)(2,1)} %bitcast.118, bf16[64,128,128]{1,2,0:T(8,128)(2,1)} %all-gather.10.cloned.1.call-done), kind=kOutput, calls=%fused_computation.48 | convolution fusion | flops 538968064 | bytes 10485760 | tf_op jit(solution)/shard_map/bmc,bmr->bcr/dot_general | solution.py:71
  53.9 151.5 %all-gather.8.cloned.1.call-done = bf16[3,32,2,2,128,128]{5,4,3,2,1,0:T(8,128)(2,1)} async-done(((bf16[3,32,2,2,64,128]{5,4,3,2,1,0:T(8,128)(2,1)}), bf16[3,32,2,2,128,128]{5,4,3,2,1,0:T(8,128)(2,1)}) %all-gather.8.cloned.1.call-update) | async-done | bytes 12582928 | tf_op jit(solution)/shard_map/all_gather | solution.py:68
  205.4 5.4 %fusion.61 = (bf16[1,32,2,2,128,128]{5,4,3,2,1,0:T(8,128)(2,1)}, bf16[1,32,2,2,128,128]{5,4,3,2,1,0:T(8,128)(2,1)S(1)}) fusion(bf16[3,32,2,2,128,128]{5,4,3,2,1,0:T(8,128)(2,1)} %all-gather.8.cloned.1.call-done), kind=kLoop, calls=%fused_computation.57 | loop fusion | bytes 16777216 | tf_op jit(solution)/shard_map/slice | solution.py:76
  211.5 3.5 bitcast_convert_fusion.5
  215.0 3.6 fusion.10
  218.6 6.9 %copy.17 = bf16[16,2,2,256,128]{4,3,2,1,0:T(8,128)(2,1)} copy(bf16[16,2,2,256,128]{3,4,1,2,0:T(8,128)(2,1)} %fusion.10) | data formatting | bytes 8388608 | tf_op jit(solution)/shard_map/convert_element_type | solution.py:40
  225.6 7.4 %fusion.11 = bf16[8,2,4,256,128]{3,4,1,2,0:T(8,128)(2,1)} fusion(bf16[8,2,4,256,128,1]{4,3,2,1,0,5:T(8,128)(2,1)} %bitcast.123, bf16[8,4,2,2,128,128]{5,4,3,2,1,0:T(8,128)(2,1)} %bitcast.126, f32[8,4,2,2,128]{4,3,2,1,0:T(2,128)S(1)} %bitcast.133), kind=kOutput, calls=%fused_computation.26 | convolution fusion | flops 1082130432 | bytes 12648448 | tf_op jit(solution)/shard_map/hclnr,hlocsr->holns/dot_general | solution.py:39
  233.0 6.5 %copy.19 = bf16[8,2,4,256,128]{4,3,2,1,0:T(8,128)(2,1)} copy(bf16[8,2,4,256,128]{3,4,1,2,0:T(8,128)(2,1)} %fusion.11) | data formatting | bytes 8388608 | tf_op jit(solution)/shard_map/convert_element_type | solution.py:40
  239.5 10.7 %all-to-all-start = ((bf16[64,256,128]{2,1,0:T(8,128)(2,1)}), bf16[64,256,128]{2,1,0:T(8,128)(2,1)}, u32[]{:S(2)}, u32[]{:S(2)}) async-start(bf16[64,256,128]{2,1,0:T(8,128)(2,1)} %bitcast.121), calls=%async_computation | async-start | bytes 8388608 | tf_op jit(solution)/shard_map/all_to_all | solution.py:84
  252.4 3.5 collective-permute-start
  258.5 13.0 %collective-permute-done = bf16[2,128,256]{2,1,0:T(8,128)(2,1)S(1)} collective-permute-done((bf16[2,128,256]{2,1,0:T(8,128)(2,1)S(1)}, bf16[2,128,256]{2,1,0:T(8,128)(2,1)S(1)}, u32[]{:S(2)}, u32[]{:S(2)}) %collective-permute-start) | collective-permute-done | bytes 131104 | tf_op jit(solution)/shard_map/ppermute | solution.py:19
  273.7 4.0 pad_maximum_fusion
  277.7 8.8 %gather_fusion = bf16[128,128,256]{2,1,0:T(8,128)(2,1)} fusion(bf16[68,128,256]{2,1,0:T(8,128)(2,1)} %pad_maximum_fusion, s32[1024]{0:T(1024)S(1)} %pad_clamp_fusion), kind=kCustom, calls=%fused_computation | custom fusion | bytes 16777728 | tf_op jit(solution)/shard_map/jit(_take)/gather | solution.py:80
  286.5 121.5 %all-gather.6.cloned.1.call-done = bf16[3,32,2,2,128,128]{5,4,3,2,1,0:T(8,128)(2,1)} async-done(((bf16[3,32,2,2,64,128]{5,4,3,2,1,0:T(8,128)(2,1)}), bf16[3,32,2,2,128,128]{5,4,3,2,1,0:T(8,128)(2,1)}) %all-gather.6.cloned.1.call-update) | async-done | bytes 12582928 | tf_op jit(solution)/shard_map/all_gather | solution.py:69
  408.0 6.2 %fusion.60 = (bf16[1,32,2,2,128,128]{5,4,3,2,1,0:T(8,128)(2,1)}, bf16[1,32,2,2,128,128]{5,4,3,2,1,0:T(8,128)(2,1)}) fusion(bf16[3,32,2,2,128,128]{5,4,3,2,1,0:T(8,128)(2,1)} %all-gather.6.cloned.1.call-done), kind=kLoop, calls=%fused_computation.56 | loop fusion | bytes 16777216 | tf_op jit(solution)/shard_map/slice | solution.py:87
  414.2 4.9 bitcast_convert_fusion.2
  422.4 6.6 %copy.21 = bf16[16,2,2,256,128]{4,3,2,1,0:T(8,128)(2,1)} copy(bf16[16,2,2,256,128]{3,4,1,2,0:T(8,128)(2,1)} %fusion.12) | data formatting | bytes 8388608 | tf_op jit(solution)/shard_map/convert_element_type | solution.py:40
  429.0 6.7 %fusion.13 = bf16[8,2,4,256,128]{3,4,1,2,0:T(8,128)(2,1)} fusion(bf16[8,2,4,256,128,1]{4,3,2,1,0,5:T(8,128)(2,1)} %bitcast.124, bf16[8,4,2,2,128,128]{5,4,3,2,1,0:T(8,128)(2,1)} %bitcast.125, f32[8,4,2,2,128]{4,3,2,1,0:T(2,128)S(1)} %bitcast.131), kind=kOutput, calls=%fused_computation.28 | convolution fusion | flops 1082130432 | bytes 12648448 | tf_op jit(solution)/shard_map/hclnr,hlocsr->holns/dot_general | solution.py:39
  435.7 6.4 %copy.23 = bf16[8,2,4,256,128]{4,3,2,1,0:T(8,128)(2,1)} copy(bf16[8,2,4,256,128]{3,4,1,2,0:T(8,128)(2,1)} %fusion.13) | data formatting | bytes 8388608 | tf_op jit(solution)/shard_map/convert_element_type | solution.py:40
  442.1 6.1 %all-gather.12.cloned.1.call-done = bf16[64,128,128]{1,2,0:T(8,128)(2,1)} async-done(((bf16[64,128,64]{1,2,0:T(8,128)(2,1)}), bf16[64,128,128]{1,2,0:T(8,128)(2,1)}) %all-gather.12.cloned.1.call-update) | async-done | bytes 2097168 | tf_op jit(solution)/shard_map/all_gather | solution.py:64
  448.3 7.4 %fusion.65 = f32[64,256,128]{1,2,0:T(8,128)} fusion(bf16[64,256,128]{2,1,0:T(8,128)(2,1)} %bitcast.120, bf16[64,128,128]{1,2,0:T(8,128)(2,1)} %all-gather.12.cloned.1.call-done), kind=kOutput, calls=%fused_computation.61 | convolution fusion | flops 536870912 | bytes 14680064 | tf_op jit(solution)/shard_map/bmr,bcr->bmc/dot_general | solution.py:89
  455.7 54.3 %all-gather.14.cloned.1.call-done = bf16[64,2,128,128]{2,3,1,0:T(8,128)(2,1)} async-done(((bf16[64,2,128,64]{2,3,1,0:T(8,128)(2,1)}), bf16[64,2,128,128]{2,3,1,0:T(8,128)(2,1)}) %all-gather.14.cloned.1.call-update) | async-done | bytes 4194320 | tf_op jit(solution)/shard_map/all_gather | solution.py:65
  510.0 10.1 %fusion.6 = bf16[64,256,128]{1,2,0:T(8,128)(2,1)} fusion(f32[64,256,128]{1,2,0:T(8,128)} %fusion.65, bf16[64,2,128,128]{2,3,1,0:T(8,128)(2,1)} %all-gather.14.cloned.1.call-done, bf16[64,2,128,256]{3,2,1,0:T(8,128)(2,1)} %bitcast.117, pred[64,2]{1,0:T(8,128)(4,1)S(1)} %copy.24), kind=kOutput, calls=%fused_computation.14 | convolution fusion | flops 1082130432 | bytes 25165952 | tf_op jit(solution)/shard_map/bkmn,bknc->bmc/dot_general | solution.py:81
  (33 shorter events, 13.2 us)
Async XLA Ops:
  6.5 41.1 %all-gather.10.cloned.1.call-start = ((), (), s32[]{:S(2)}) async-start(), calls=%async_computation.3 | async-start | bytes 3145728 | tf_op jit(solution)/shard_map/all_gather | solution.py:63
  7.3 198.1 %all-gather.8.cloned.1.call-start = ((), (), s32[]{:S(2)}) async-start(), calls=%async_computation.2 | async-start | bytes 18874368 | tf_op jit(solution)/shard_map/all_gather | solution.py:68
  8.0 0.9 copy-start.2
  8.0 400.0 %all-gather.6.cloned.1.call-start = ((), (), s32[]{:S(2)}) async-start(), calls=%async_computation.1 | async-start | bytes 18874368 | tf_op jit(solution)/shard_map/all_gather | solution.py:69
  205.4 6.2 %copy-start = (bf16[64,256,128]{2,1,0:T(8,128)(2,1)S(1)}, bf16[64,256,128]{2,1,0:T(8,128)(2,1)}, u32[]{:S(2)}) copy-start(bf16[64,256,128]{2,1,0:T(8,128)(2,1)} %convolution_convert_fusion) | copy-start | bytes 12582916
  239.5 18.6 %copy-start.3 = (f32[3,32,2,2,128]{4,3,2,1,0:T(2,128)S(1)}, f32[3,32,2,2,128]{4,3,2,1,0:T(2,128)}, u32[]{:S(2)}) copy-start(f32[3,32,2,2,128]{4,3,2,1,0:T(2,128)} %param.17) | copy-start | bytes 589828
  239.5 18.6 %copy-start.4 = (s32[64,2]{0,1:T(2,128)S(1)}, s32[64,2]{0,1:T(2,128)}, u32[]{:S(2)}) copy-start(s32[64,2]{0,1:T(2,128)} %param.13) | copy-start | bytes 1540
  239.5 174.7 %all-to-all-start = ((bf16[64,256,128]{2,1,0:T(8,128)(2,1)}), bf16[64,256,128]{2,1,0:T(8,128)(2,1)}, u32[]{:S(2)}, u32[]{:S(2)}) async-start(bf16[64,256,128]{2,1,0:T(8,128)(2,1)} %bitcast.121), calls=%async_computation | async-start | bytes 8388608 | tf_op jit(solution)/shard_map/all_to_all | solution.py:84
  250.3 198.0 %all-gather.12.cloned.1.call-start = ((), (), s32[]{:S(2)}) async-start(), calls=%async_computation.4 | async-start | bytes 3145728 | tf_op jit(solution)/shard_map/all_gather | solution.py:64
  250.8 259.2 %all-gather.14.cloned.1.call-start = ((), (), s32[]{:S(2)}) async-start(), calls=%async_computation.5 | async-start | bytes 6291456 | tf_op jit(solution)/shard_map/all_gather | solution.py:65
  252.4 19.1 %collective-permute-start = (bf16[2,128,256]{2,1,0:T(8,128)(2,1)S(1)}, bf16[2,128,256]{2,1,0:T(8,128)(2,1)S(1)}, u32[]{:S(2)}, u32[]{:S(2)}) collective-permute-start(bf16[2,128,256]{2,1,0:T(8,128)(2,1)S(1)} %bitcast.130), channel_id=1, source_target_pairs={{0,2},{2,4},{4,6},{6,8},{8,10},{10,12},{12,14},{14,16},{16,18},{18... | collective-permute-start | bytes 393224 | tf_op jit(solution)/shard_map/ppermute | solution.py:19
  256.0 17.8 %collective-permute-start.1 = (bf16[2,128,256]{2,1,0:T(8,128)(2,1)S(1)}, bf16[2,128,256]{2,1,0:T(8,128)(2,1)S(1)}, u32[]{:S(2)}, u32[]{:S(2)}) collective-permute-start(bf16[2,128,256]{2,1,0:T(8,128)(2,1)S(1)} %bitcast.129), channel_id=1, source_target_pairs={{2,0},{4,2},{6,4},{8,6},{10,8},{12,10},{14,12},{16,14},{18,16},{20... | collective-permute-start | bytes 393224 | tf_op jit(solution)/shard_map/ppermute | solution.py:21
  414.2 4.9 copy-start.1
Sparse Core Ops, SparseCore 0:
  9.0 38.6 all-gather.9
  49.3 155.9 all-gather.7
  207.0 200.9 all-gather.5
  409.5 38.7 all-gather.11
  449.8 60.2 all-gather.13
where the time goes:
time: 528 us; the launch traced here: 527 us
  waiting for transfers between devices  391 us (74%)
  matrix products  53.1 us (10%)
  local copies, waits for them, and re-layouts  49.3 us (9%)
  starting transfers between devices  16.5 us (3%)
  between operations  13.3 us (3%)
    all_gather x1, waiting for transfers between devices, on_device(): lax.all_gather(source_values, 'rhs', axis=4, tiled=True)  152 us
    all_gather x1, waiting for transfers between devices, on_device(): lax.all_gather(target_values, 'rhs', axis=4, tiled=True)  121 us
    all_gather x1, waiting for transfers between devices, on_device(): lax.all_gather(near_blocks, 'rhs', axis=3, tiled=True)  54.3 us
    all_gather x1, waiting for transfers between devices, on_device(): lax.all_gather(source_basis, 'rhs', axis=2, tiled=True)  38.7 us
    dot_general x6, matrix products, butterfly_level(): jnp.einsum('hclnr,hlocsr->holns', inputs, matrices, preferred_element_typ...  29.3 us
    convert_element_type x4, local copies, waits for them, and re-layouts, butterfly_level(): return mixed.reshape(box_total, columns, outputs).astype(jnp.bfloat16)  26.5 us
    ppermute x1, waiting for transfers between devices, padded_2(): lax.ppermute(tail, axis, [(i, (i + 1) % count) for i in range(ends)])  13 us
    all_to_all x1, starting transfers between devices, on_device(): lax.all_to_all(coefficients, 'leaf', split_axis=0, concat_axis=0, tiled=T...  10.7 us
  transfers between devices with their start and end apart: 8, of which 7 were waited for; matrix products, arithmetic and copies ran while one was open for 18% of the time, Pallas kernels for 0%

commit v1 on v0

--- a/solution.py
+++ b/solution.py
@@ -60,7 +60,7 @@
     columns = rhs.shape[1]
     rhs_boxes = rhs.reshape(box_count, box_rows, columns)
     basis_in, basis_out, near_full = (
-        lax.all_gather(source_basis, "rhs", axis=2, tiled=True),
+        jnp.concatenate(lax.all_gather(source_basis, "rhs"), axis=2),
         lax.all_gather(target_basis, "rhs", axis=2, tiled=True),
         lax.all_gather(near_blocks, "rhs", axis=3, tiled=True),
     )

time: 528 us -> 528 us (level)
  no operation moved by 1% of the time
where the time goes in v1:
time: 528 us; the launch traced here: 527 us
  waiting for transfers between devices  390 us (74%)
  local copies, waits for them, and re-layouts  52.1 us (10%)
  matrix products  50.2 us (10%)
  starting transfers between devices  16.5 us (3%)
  between operations  13.3 us (3%)
    all_gather x1, waiting for transfers between devices, on_device(): lax.all_gather(source_values, 'rhs', axis=4, tiled=True)  152 us
    all_gather x1, waiting for transfers between devices, on_device(): lax.all_gather(target_values, 'rhs', axis=4, tiled=True)  121 us
    all_gather x1, waiting for transfers between devices, on_device(): lax.all_gather(near_blocks, 'rhs', axis=3, tiled=True)  54.3 us
    all_gather x1, waiting for transfers between devices, on_device(): lax.all_gather(source_basis, 'rhs')  38.7 us
    dot_general x6, matrix products, butterfly_level(): jnp.einsum('hclnr,hlocsr->holns', inputs, matrices, preferred_element_typ...  29.3 us
    convert_element_type x4, local copies, waits for them, and re-layouts, butterfly_level(): return mixed.reshape(box_total, columns, outputs).astype(jnp.bfloat16)  26.6 us
    ppermute x1, waiting for transfers between devices, padded_2(): lax.ppermute(tail, axis, [(i, (i + 1) % count) for i in range(ends)])  13 us
    all_to_all x1, starting transfers between devices, on_device(): lax.all_to_all(coefficients, 'leaf', split_axis=0, concat_axis=0, tiled=T...  10.7 us
  transfers between devices with their start and end apart: 8, of which 7 were waited for; matrix products, arithmetic and copies ran while one was open for 18% of the time, Pallas kernels for 0%

profile of v1, /device:TPU:1, one launch (start us, length us, event | category | flops | bytes accessed | tf_op | source)
XLA Modules:
  0.0 526.6 jit_solution(7762502982556161275)
XLA Ops:
  9.0 38.7 %all-gather.15.cloned.1.call-done = bf16[128,128,64]{1,2,0:T(8,128)(2,1)} async-done(((bf16[64,128,64]{1,2,0:T(8,128)(2,1)}), bf16[128,128,64]{1,2,0:T(8,128)(2,1)}) %all-gather.15.cloned.1.call-update) | async-done | bytes 2097168 | tf_op jit(solution)/shard_map/all_gather | solution.py:63
  50.5 3.3 convolution_convert_fusion
  53.8 151.6 %all-gather.9.cloned.1.call-done = bf16[3,32,2,2,128,128]{5,4,3,2,1,0:T(8,128)(2,1)} async-done(((bf16[3,32,2,2,64,128]{5,4,3,2,1,0:T(8,128)(2,1)}), bf16[3,32,2,2,128,128]{5,4,3,2,1,0:T(8,128)(2,1)}) %all-gather.9.cloned.1.call-update) | async-done | bytes 12582928 | tf_op jit(solution)/shard_map/all_gather | solution.py:68
  205.4 5.4 %fusion.61 = (bf16[1,32,2,2,128,128]{5,4,3,2,1,0:T(8,128)(2,1)}, bf16[1,32,2,2,128,128]{5,4,3,2,1,0:T(8,128)(2,1)S(1)}) fusion(bf16[3,32,2,2,128,128]{5,4,3,2,1,0:T(8,128)(2,1)} %all-gather.9.cloned.1.call-done), kind=kLoop, calls=%fused_computation.57 | loop fusion | bytes 16777216 | tf_op jit(solution)/shard_map/slice | solution.py:76
  211.5 3.5 bitcast_convert_fusion.5
  215.0 3.6 fusion.10
  218.6 7.0 %copy.45 = bf16[16,2,2,256,128]{4,3,2,1,0:T(8,128)(2,1)} copy(bf16[16,2,2,256,128]{3,4,1,2,0:T(8,128)(2,1)} %fusion.10) | data formatting | bytes 8388608 | tf_op jit(solution)/shard_map/convert_element_type | solution.py:40
  225.6 7.4 %fusion.11 = bf16[8,2,4,256,128]{3,4,1,2,0:T(8,128)(2,1)} fusion(bf16[8,2,4,256,128,1]{4,3,2,1,0,5:T(8,128)(2,1)} %bitcast.128, bf16[8,4,2,2,128,128]{5,4,3,2,1,0:T(8,128)(2,1)} %bitcast.131, f32[8,4,2,2,128]{4,3,2,1,0:T(2,128)S(1)} %bitcast.139), kind=kOutput, calls=%fused_computation.26 | convolution fusion | flops 1082130432 | bytes 12648448 | tf_op jit(solution)/shard_map/hclnr,hlocsr->holns/dot_general | solution.py:39
  233.0 6.6 %copy.47 = bf16[8,2,4,256,128]{4,3,2,1,0:T(8,128)(2,1)} copy(bf16[8,2,4,256,128]{3,4,1,2,0:T(8,128)(2,1)} %fusion.11) | data formatting | bytes 8388608 | tf_op jit(solution)/shard_map/convert_element_type | solution.py:40
  239.6 10.7 %all-to-all-start = ((bf16[64,256,128]{2,1,0:T(8,128)(2,1)}), bf16[64,256,128]{2,1,0:T(8,128)(2,1)}, u32[]{:S(2)}, u32[]{:S(2)}) async-start(bf16[64,256,128]{2,1,0:T(8,128)(2,1)} %bitcast.125), calls=%async_computation | async-start | bytes 8388608 | tf_op jit(solution)/shard_map/all_to_all | solution.py:84
  252.5 3.5 collective-permute-start
  258.5 13.0 %collective-permute-done = bf16[2,128,256]{2,1,0:T(8,128)(2,1)S(1)} collective-permute-done((bf16[2,128,256]{2,1,0:T(8,128)(2,1)S(1)}, bf16[2,128,256]{2,1,0:T(8,128)(2,1)S(1)}, u32[]{:S(2)}, u32[]{:S(2)}) %collective-permute-start) | collective-permute-done | bytes 131104 | tf_op jit(solution)/shard_map/ppermute | solution.py:19
  273.8 4.1 pad_maximum_fusion
  277.9 8.8 %gather_fusion = bf16[128,128,256]{2,1,0:T(8,128)(2,1)} fusion(bf16[68,128,256]{2,1,0:T(8,128)(2,1)} %pad_maximum_fusion, s32[1024]{0:T(1024)S(1)} %pad_clamp_fusion), kind=kCustom, calls=%fused_computation | custom fusion | bytes 16777728 | tf_op jit(solution)/shard_map/jit(_take)/gather | solution.py:80
  286.7 121.3 %all-gather.7.cloned.1.call-done = bf16[3,32,2,2,128,128]{5,4,3,2,1,0:T(8,128)(2,1)} async-done(((bf16[3,32,2,2,64,128]{5,4,3,2,1,0:T(8,128)(2,1)}), bf16[3,32,2,2,128,128]{5,4,3,2,1,0:T(8,128)(2,1)}) %all-gather.7.cloned.1.call-update) | async-done | bytes 12582928 | tf_op jit(solution)/shard_map/all_gather | solution.py:69
  408.0 6.2 %fusion.60 = (bf16[1,32,2,2,128,128]{5,4,3,2,1,0:T(8,128)(2,1)}, bf16[1,32,2,2,128,128]{5,4,3,2,1,0:T(8,128)(2,1)}) fusion(bf16[3,32,2,2,128,128]{5,4,3,2,1,0:T(8,128)(2,1)} %all-gather.7.cloned.1.call-done), kind=kLoop, calls=%fused_computation.56 | loop fusion | bytes 16777216 | tf_op jit(solution)/shard_map/slice | solution.py:87
  414.2 4.9 bitcast_convert_fusion.2
  422.4 6.6 %copy.49 = bf16[16,2,2,256,128]{4,3,2,1,0:T(8,128)(2,1)} copy(bf16[16,2,2,256,128]{3,4,1,2,0:T(8,128)(2,1)} %fusion.12) | data formatting | bytes 8388608 | tf_op jit(solution)/shard_map/convert_element_type | solution.py:40
  429.0 6.7 %fusion.13 = bf16[8,2,4,256,128]{3,4,1,2,0:T(8,128)(2,1)} fusion(bf16[8,2,4,256,128,1]{4,3,2,1,0,5:T(8,128)(2,1)} %bitcast.129, bf16[8,4,2,2,128,128]{5,4,3,2,1,0:T(8,128)(2,1)} %bitcast.130, f32[8,4,2,2,128]{4,3,2,1,0:T(2,128)S(1)} %bitcast.137), kind=kOutput, calls=%fused_computation.28 | convolution fusion | flops 1082130432 | bytes 12648448 | tf_op jit(solution)/shard_map/hclnr,hlocsr->holns/dot_general | solution.py:39
  435.7 6.4 %copy.51 = bf16[8,2,4,256,128]{4,3,2,1,0:T(8,128)(2,1)} copy(bf16[8,2,4,256,128]{3,4,1,2,0:T(8,128)(2,1)} %fusion.13) | data formatting | bytes 8388608 | tf_op jit(solution)/shard_map/convert_element_type | solution.py:40
  442.1 6.1 %all-gather.11.cloned.1.call-done = bf16[64,128,128]{1,2,0:T(8,128)(2,1)} async-done(((bf16[64,128,64]{1,2,0:T(8,128)(2,1)}), bf16[64,128,128]{1,2,0:T(8,128)(2,1)}) %all-gather.11.cloned.1.call-update) | async-done | bytes 2097168 | tf_op jit(solution)/shard_map/all_gather | solution.py:64
  448.3 7.4 %fusion.65 = f32[64,256,128]{1,2,0:T(8,128)} fusion(bf16[64,256,128]{2,1,0:T(8,128)(2,1)} %bitcast.124, bf16[64,128,128]{1,2,0:T(8,128)(2,1)} %all-gather.11.cloned.1.call-done), kind=kOutput, calls=%fused_computation.61 | convolution fusion | flops 536870912 | bytes 14680064 | tf_op jit(solution)/shard_map/bmr,bcr->bmc/dot_general | solution.py:89
  455.7 54.3 %all-gather.13.cloned.1.call-done = bf16[64,2,128,128]{2,3,1,0:T(8,128)(2,1)} async-done(((bf16[64,2,128,64]{2,3,1,0:T(8,128)(2,1)}), bf16[64,2,128,128]{2,3,1,0:T(8,128)(2,1)}) %all-gather.13.cloned.1.call-update) | async-done | bytes 4194320 | tf_op jit(solution)/shard_map/all_gather | solution.py:65
  510.0 10.1 %fusion.6 = bf16[64,256,128]{1,2,0:T(8,128)(2,1)} fusion(f32[64,256,128]{1,2,0:T(8,128)} %fusion.65, bf16[64,2,128,128]{2,3,1,0:T(8,128)(2,1)} %all-gather.13.cloned.1.call-done, bf16[64,2,128,256]{3,2,1,0:T(8,128)(2,1)} %bitcast.121, pred[64,2]{1,0:T(8,128)(4,1)S(1)} %copy.52), kind=kOutput, calls=%fused_computation.14 | convolution fusion | flops 1082130432 | bytes 25165952 | tf_op jit(solution)/shard_map/bkmn,bknc->bmc/dot_general | solution.py:81
  (36 shorter events, 16.0 us)
Async XLA Ops:
  6.5 41.1 %all-gather.15.cloned.1.call-start = ((), (), s32[]{:S(2)}) async-start(), calls=%async_computation.5 | async-start | bytes 3145728 | tf_op jit(solution)/shard_map/all_gather | solution.py:63
  7.3 198.1 %all-gather.9.cloned.1.call-start = ((), (), s32[]{:S(2)}) async-start(), calls=%async_computation.2 | async-start | bytes 18874368 | tf_op jit(solution)/shard_map/all_gather | solution.py:68
  8.0 0.9 copy-start.3
  8.0 400.0 %all-gather.7.cloned.1.call-start = ((), (), s32[]{:S(2)}) async-start(), calls=%async_computation.1 | async-start | bytes 18874368 | tf_op jit(solution)/shard_map/all_gather | solution.py:69
  47.7 2.8 copy-start
  205.4 6.2 %copy-start.1 = (bf16[64,256,128]{2,1,0:T(8,128)(2,1)S(1)}, bf16[64,256,128]{2,1,0:T(8,128)(2,1)}, u32[]{:S(2)}) copy-start(bf16[64,256,128]{2,1,0:T(8,128)(2,1)} %convolution_convert_fusion) | copy-start | bytes 12582916
  239.6 18.6 %copy-start.4 = (f32[3,32,2,2,128]{4,3,2,1,0:T(2,128)S(1)}, f32[3,32,2,2,128]{4,3,2,1,0:T(2,128)}, u32[]{:S(2)}) copy-start(f32[3,32,2,2,128]{4,3,2,1,0:T(2,128)} %param.17) | copy-start | bytes 589828
  239.6 18.6 %copy-start.5 = (s32[64,2]{0,1:T(2,128)S(1)}, s32[64,2]{0,1:T(2,128)}, u32[]{:S(2)}) copy-start(s32[64,2]{0,1:T(2,128)} %param.13) | copy-start | bytes 1540
  239.6 174.6 %all-to-all-start = ((bf16[64,256,128]{2,1,0:T(8,128)(2,1)}), bf16[64,256,128]{2,1,0:T(8,128)(2,1)}, u32[]{:S(2)}, u32[]{:S(2)}) async-start(bf16[64,256,128]{2,1,0:T(8,128)(2,1)} %bitcast.125), calls=%async_computation | async-start | bytes 8388608 | tf_op jit(solution)/shard_map/all_to_all | solution.py:84
  250.3 198.0 %all-gather.11.cloned.1.call-start = ((), (), s32[]{:S(2)}) async-start(), calls=%async_computation.3 | async-start | bytes 3145728 | tf_op jit(solution)/shard_map/all_gather | solution.py:64
  250.9 259.1 %all-gather.13.cloned.1.call-start = ((), (), s32[]{:S(2)}) async-start(), calls=%async_computation.4 | async-start | bytes 6291456 | tf_op jit(solution)/shard_map/all_gather | solution.py:65
  252.5 19.1 %collective-permute-start = (bf16[2,128,256]{2,1,0:T(8,128)(2,1)S(1)}, bf16[2,128,256]{2,1,0:T(8,128)(2,1)S(1)}, u32[]{:S(2)}, u32[]{:S(2)}) collective-permute-start(bf16[2,128,256]{2,1,0:T(8,128)(2,1)S(1)} %bitcast.136), channel_id=1, source_target_pairs={{0,2},{2,4},{4,6},{6,8},{8,10},{10,12},{12,14},{14,16},{16,18},{18... | collective-permute-start | bytes 393224 | tf_op jit(solution)/shard_map/ppermute | solution.py:19
  256.0 17.8 %collective-permute-start.1 = (bf16[2,128,256]{2,1,0:T(8,128)(2,1)S(1)}, bf16[2,128,256]{2,1,0:T(8,128)(2,1)S(1)}, u32[]{:S(2)}, u32[]{:S(2)}) collective-permute-start(bf16[2,128,256]{2,1,0:T(8,128)(2,1)S(1)} %bitcast.135), channel_id=1, source_target_pairs={{2,0},{4,2},{6,4},{8,6},{10,8},{12,10},{14,12},{16,14},{18,16},{20... | collective-permute-start | bytes 393224 | tf_op jit(solution)/shard_map/ppermute | solution.py:21
  414.2 4.9 copy-start.2
Sparse Core Ops, SparseCore 0:
  9.0 38.6 all-gather.14
  49.3 155.9 all-gather.8
  207.0 200.9 all-gather.6
  409.5 38.7 all-gather.10
  449.8 60.2 all-gather.12
